TPU v7x, 256 devices: a whole 4x4x8 slice. The times are simulated.
256 devices in a mesh: dp: 2 (over z_lo), expert: 128 (over y, x, z_hi, core).
Axes of the slice: x: 4, y: 4, z: 8 (z_hi: 4, z_lo: 2; z = z_hi * 2 + z_lo), core: 2. Of those that a mesh axis runs over, the one named last changes fastest.
Arguments:
- tokens: bfloat16 [32768, 4096], P(('dp', 'expert')), may hold values from -6 to 6
- routes: int32 [256, 16, 4], P(('dp', 'expert')), may hold values from 0 to 127, as said below
- gate_values: float32 [256, 16, 4], P(('dp', 'expert')), may hold values from 0.1 to 1
- gate_weight: bfloat16 [128, 4096, 256], P('expert', 'dp'), may hold values from -0.09375 to 0.09375
- up_weight: bfloat16 [128, 4096, 256], P('expert', 'dp'), may hold values from -0.09375 to 0.09375
- down_weight: bfloat16 [128, 4096, 256], P('expert', 'dp'), may hold values from -0.125 to 0.125
- cotangent: bfloat16 [32768, 4096], P(('dp', 'expert')), may hold values from -6 to 6
Outputs:
- layer_out: bfloat16 [32768, 4096], P(('dp', 'expert'))
- token_grad: bfloat16 [32768, 4096], P(('dp', 'expert'))
- gate_grad: bfloat16 [128, 4096, 256], P('expert', 'dp')
- up_grad: bfloat16 [128, 4096, 256], P('expert', 'dp')
- down_grad: bfloat16 [128, 4096, 256], P('expert', 'dp')
Inputs may be any that keep to these rules, and one draw needn't show every extreme that they name: `routes`: for each home block and each expert, 4 distinct positions within that block.
All inputs are finite; a program needn't handle non-finite values.
Results may differ from a plain program's by a relative error of at most 0.025.
Values may be sent and summed in bfloat16 or wider, within the bound.
A program may use at most 128 MiB of HBM per device.

v0:
```python
import jax
import jax.numpy as jnp
from jax import lax
from jax.sharding import Mesh
from jax.sharding import PartitionSpec as P

SPLIT = 8
ROWS = ("dp", "yx", "col")


def send_out(payload):
    arrived = lax.all_to_all(payload, "yx", split_axis=0, concat_axis=0, tiled=True)
    shared = lax.all_gather(arrived, "col", axis=0, tiled=True)
    return shared.reshape(-1, payload.shape[-1])


def bring_back(partial_value, expert_count):
    total_rows, width = partial_value.shape
    summed = lax.psum_scatter(partial_value, "col", scatter_dimension=0, tiled=True)
    summed = summed.reshape(expert_count, -1, width)
    returned = lax.all_to_all(summed, "yx", split_axis=0, concat_axis=0, tiled=True)
    return returned.astype(jnp.float32)


def shards(tokens, routes, gate_values, gate_weight, up_weight, down_weight, cotangent):
    width = tokens.shape[1]
    expert_count = routes.shape[1]
    chosen = routes[0]
    scales = gate_values[0][:, :, None]
    contract_last = (((1,), (1,)), ((), ()))
    contract_first = (((0,), (0,)), ((), ()))
    full_gate, full_up, full_down = (
        lax.all_gather(gate_weight, "dp", axis=1, tiled=True),
        lax.all_gather(up_weight, "dp", axis=1, tiled=True),
        lax.all_gather(down_weight, "dp", axis=1, tiled=True),
    )
    full_gate = full_gate[0]
    full_up = full_up[0]
    full_down = full_down[0]
    token_rows = send_out(tokens[chosen])
    scaled_cot = (scales * cotangent[chosen].astype(jnp.float32)).astype(jnp.bfloat16)
    cot_rows = send_out(scaled_cot)
    gate_pre = jnp.dot(token_rows, full_gate, preferred_element_type=jnp.float32)
    up_pre = jnp.dot(token_rows, full_up, preferred_element_type=jnp.float32)
    gate_sigma = jax.nn.sigmoid(gate_pre)
    hidden = (gate_pre * gate_sigma * up_pre).astype(jnp.bfloat16)
    partial_value = lax.dot_general(
        hidden, full_down, contract_last, preferred_element_type=jnp.float32
    ).astype(jnp.bfloat16)
    combined = bring_back(partial_value, expert_count)
    layer_out = jnp.zeros((tokens.shape[0], width), jnp.float32).at[chosen].add(scales * combined)
    hidden_grad = jnp.dot(cot_rows, full_down, preferred_element_type=jnp.float32)
    gate_rows = (hidden_grad * up_pre * gate_sigma * (1.0 + gate_pre * (1.0 - gate_sigma))).astype(
        jnp.bfloat16
    )
    up_rows = (hidden_grad * gate_pre * gate_sigma).astype(jnp.bfloat16)
    partial_grad = (
        lax.dot_general(gate_rows, full_gate, contract_last, preferred_element_type=jnp.float32)
        + lax.dot_general(up_rows, full_up, contract_last, preferred_element_type=jnp.float32)
    ).astype(jnp.bfloat16)
    token_grad = (
        jnp.zeros((tokens.shape[0], width), jnp.float32)
        .at[chosen]
        .add(bring_back(partial_grad, expert_count))
    )
    grad_sums = lax.psum_scatter(
        jnp.concatenate(
            [
                lax.dot_general(
                    token_rows, gate_rows, contract_first, preferred_element_type=jnp.float32
                ),
                lax.dot_general(
                    token_rows, up_rows, contract_first, preferred_element_type=jnp.float32
                ),
                lax.dot_general(
                    cot_rows, hidden, contract_first, preferred_element_type=jnp.float32
                ),
            ],
            axis=1,
        ).astype(jnp.bfloat16),
        "dp",
        scatter_dimension=0,
        tiled=True,
    ).astype(jnp.float32)
    hidden_width = hidden.shape[1]
    gate_grad = grad_sums[:, :hidden_width].astype(jnp.bfloat16)[None]
    up_grad = grad_sums[:, hidden_width : 2 * hidden_width].astype(jnp.bfloat16)[None]
    down_grad = grad_sums[:, 2 * hidden_width :].astype(jnp.bfloat16)[None]
    return (
        layer_out.astype(jnp.bfloat16),
        token_grad.astype(jnp.bfloat16),
        gate_grad,
        up_grad,
        down_grad,
    )


def solution(mesh):
    n_dp, n_expert = mesh.devices.shape
    fine = Mesh(mesh.devices.reshape(n_dp, n_expert // SPLIT, SPLIT), ROWS)
    placed = (
        P(ROWS, None),
        P(ROWS, None, None),
        P(ROWS, None, None),
        P(("yx", "col"), "dp", None),
        P(("yx", "col"), "dp", None),
        P(("yx", "col"), "dp", None),
        P(ROWS, None),
    )
    return jax.shard_map(
        shards,
        mesh=fine,
        in_specs=placed,
        out_specs=(
            P(ROWS, None),
            P(ROWS, None),
            P(("yx", "col"), "dp", None),
            P(("yx", "col"), "dp", None),
            P(("yx", "col"), "dp", None),
        ),
        check_vma=False,
    )
```

profile of v0, /device:TPU:1, one launch (start us, length us, event | category | flops | bytes accessed | tf_op | source)
XLA Modules:
  0.0 485.7 jit_solution(14935874238161383922)
XLA Ops:
  9.5 18.0 %all_to_all.20 = bf16[16,4,4096]{2,1,0:T(4,128)(2,1)} all-to-all(bf16[16,4,4096]{2,1,0:T(4,128)(2,1)S(1)} %reshape.56), channel_id=1, replica_groups=mesh['dp'=2,'yx'=16,'col'=8] {'yx'}, dimensions={0} | all-to-all | bytes 1048576 | tf_op jit(solution)/shard_map/all_to_all | solution.py:12
  29.2 13.0 %all_to_all.21 = bf16[16,4,4096]{2,1,0:T(4,128)(2,1)} all-to-all(bf16[16,4,4096]{2,1,0:T(4,128)(2,1)S(1)} %multiply_convert_fusion), channel_id=1, replica_groups=mesh['dp'=2,'yx'=16,'col'=8] {'yx'}, dimensions={0} | all-to-all | bytes 1048576 | tf_op jit(solution)/shard_map/all_to_all | solution.py:12
  44.1 34.5 %all-gather.6.cloned.1.call-done = bf16[128,4,4096]{2,1,0:T(4,128)(2,1)} async-done(((bf16[16,4,4096]{2,1,0:T(4,128)(2,1)}), bf16[128,4,4096]{2,1,0:T(4,128)(2,1)}) %all-gather.6.cloned.1.call-update) | async-done | bytes 4194320 | tf_op jit(solution)/shard_map/all_gather | solution.py:13
  78.6 6.9 %reshape.51 = bf16[512,4096]{1,0:T(8,128)(2,1)} reshape(bf16[128,4,4096]{2,1,0:T(4,128)(2,1)} %all-gather.6.cloned.1.call-done) | data formatting | bytes 8388608 | tf_op jit(solution)/shard_map/reshape | solution.py:14
  85.4 46.2 %all-gather.14.cloned.1.call-done = bf16[128,4,4096]{2,1,0:T(4,128)(2,1)} async-done(((bf16[16,4,4096]{2,1,0:T(4,128)(2,1)}), bf16[128,4,4096]{2,1,0:T(4,128)(2,1)}) %all-gather.14.cloned.1.call-update) | async-done | bytes 4194320 | tf_op jit(solution)/shard_map/all_gather | solution.py:13
  131.6 7.0 %reshape.53 = bf16[512,4096]{1,0:T(8,128)(2,1)} reshape(bf16[128,4,4096]{2,1,0:T(4,128)(2,1)} %all-gather.14.cloned.1.call-done) | data formatting | bytes 8388608 | tf_op jit(solution)/shard_map/reshape | solution.py:14
  138.6 33.8 %all-gather.10.cloned.1.call-done = bf16[1,4096,256]{2,1,0:T(8,128)(2,1)} async-done(((bf16[1,2048,256]{2,1,0:T(8,128)(2,1)}), bf16[1,4096,256]{2,1,0:T(8,128)(2,1)}) %all-gather.10.cloned.1.call-update) | async-done | bytes 2097168 | tf_op jit(solution)/shard_map/all_gather | solution.py:34
  172.4 4.1 fusion.4
  176.5 36.2 %all-gather.8.cloned.1.call-done = bf16[1,4096,256]{2,1,0:T(8,128)(2,1)} async-done(((bf16[1,2048,256]{2,1,0:T(8,128)(2,1)}), bf16[1,4096,256]{2,1,0:T(8,128)(2,1)}) %all-gather.8.cloned.1.call-update) | async-done | bytes 2097168 | tf_op jit(solution)/shard_map/all_gather | solution.py:33
  212.8 4.1 fusion.8
  216.9 36.2 %all-gather.12.cloned.1.call-done = bf16[1,4096,256]{2,1,0:T(8,128)(2,1)} async-done(((bf16[1,2048,256]{2,1,0:T(8,128)(2,1)}), bf16[1,4096,256]{2,1,0:T(8,128)(2,1)}) %all-gather.12.cloned.1.call-update) | async-done | bytes 2097168 | tf_op jit(solution)/shard_map/all_gather | solution.py:35
  253.1 4.4 multiply_convert_fusion.1
  257.5 3.4 convolution_convert_fusion
  264.1 3.3 add_convert_fusion
  267.6 3.6 convolution_convert_fusion.1
  274.0 9.4 %pad_maximum_fusion = bf16[4096,768]{0,1:T(8,128)(2,1)} fusion(bf16[4096,256]{0,1:T(8,128)(2,1)S(1)} %convolution_convert_fusion.1, bf16[4096,256]{0,1:T(8,128)(2,1)S(1)} %convolution_convert_fusion.2, bf16[4096,256]{0,1:T(8,128)(2,1)S(1)} %convolution_convert_fusion.3), kind=kLoop, calls=%fused_computation.5 | loop fusion | flops 18874368 | bytes 12582912 | tf_op jit(solution)/shard_map/concatenate | solution.py:67
  283.4 36.0 %reduce-scatter.4.cloned.1.call-done = bf16[64,4096]{1,0:T(8,128)(2,1)} async-done(((bf16[512,4096]{1,0:T(8,128)(2,1)}), bf16[64,4096]{1,0:T(8,128)(2,1)}) %reduce-scatter.4.cloned.1.call-update) | async-done | bytes 524304 | tf_op jit(solution)/shard_map/reduce_scatter | solution.py:19
  321.4 6.1 %all-to-all-start.1 = ((bf16[16,4,4096]{2,1,0:T(4,128)(2,1)}), bf16[16,4,4096]{2,1,0:T(4,128)(2,1)S(1)}, u32[]{:S(2)}, u32[]{:S(2)}) async-start(bf16[16,4,4096]{2,1,0:T(4,128)(2,1)} %reshape.52), calls=%async_computation.2 | async-start | bytes 1048576 | tf_op jit(solution)/shard_map/all_to_all | solution.py:21
  327.6 55.5 %reduce-scatter.6.cloned.1.call-done = bf16[64,4096]{1,0:T(8,128)(2,1)} async-done(((bf16[512,4096]{1,0:T(8,128)(2,1)}), bf16[64,4096]{1,0:T(8,128)(2,1)}) %reduce-scatter.6.cloned.1.call-update) | async-done | bytes 524304 | tf_op jit(solution)/shard_map/reduce_scatter | solution.py:19
  385.1 6.5 %all-to-all-start.3 = ((bf16[16,4,4096]{2,1,0:T(4,128)(2,1)}), bf16[16,4,4096]{2,1,0:T(4,128)(2,1)}, u32[]{:S(2)}, u32[]{:S(2)}) async-start(bf16[16,4,4096]{2,1,0:T(4,128)(2,1)} %reshape.54), calls=%async_computation.5 | async-start | bytes 1048576 | tf_op jit(solution)/shard_map/all_to_all | solution.py:21
  393.3 3.1 scatter_custom_fusion
  397.5 6.7 %all-to-all-done.3 = bf16[16,4,4096]{2,1,0:T(4,128)(2,1)} async-done(((bf16[16,4,4096]{2,1,0:T(4,128)(2,1)}), bf16[16,4,4096]{2,1,0:T(4,128)(2,1)}, u32[]{:S(2)}, u32[]{:S(2)}) %all-to-all-start.3) | async-done | bytes 524320 | tf_op jit(solution)/shard_map/all_to_all | solution.py:21
  408.8 62.0 %reduce-scatter.8.cloned.1.call-done = bf16[2048,768]{0,1:T(8,128)(2,1)} async-done(((bf16[4096,768]{0,1:T(8,128)(2,1)}), bf16[2048,768]{0,1:T(8,128)(2,1)}) %reduce-scatter.8.cloned.1.call-update) | async-done | bytes 3145744 | tf_op jit(solution)/shard_map/reduce_scatter | solution.py:66
  470.8 3.2 slice_bitcast_fusion
  (57 shorter events, 28.2 us)
Async XLA Ops:
  7.2 1.2 copy-start
  7.2 20.4 %copy-start.7 = (f32[1,16,4]{1,2,0:T(4,128)S(1)}, f32[1,16,4]{1,2,0:T(4,128)}, u32[]{:S(2)}) copy-start(f32[1,16,4]{1,2,0:T(4,128)} %param.9) | copy-start | bytes 772
  7.2 20.5 %copy-start.2 = (bf16[128,4096]{1,0:T(8,128)(2,1)S(1)}, bf16[128,4096]{1,0:T(8,128)(2,1)}, u32[]{:S(2)}) copy-start(bf16[128,4096]{1,0:T(8,128)(2,1)} %param.13) | copy-start | bytes 3145732
  7.2 71.3 %all-gather.6.cloned.1.call-start = ((), (), s32[]{:S(2)}) async-start(), calls=%async_computation.7 | async-start | bytes 4718592 | tf_op jit(solution)/shard_map/all_gather | solution.py:13
  27.5 104.1 %all-gather.14.cloned.1.call-start = ((), (), s32[]{:S(2)}) async-start(), calls=%async_computation.12 | async-start | bytes 4718592 | tf_op jit(solution)/shard_map/all_gather | solution.py:13
  42.2 130.3 %all-gather.10.cloned.1.call-start = ((), (), s32[]{:S(2)}) async-start(), calls=%async_computation.9 | async-start | bytes 3145728 | tf_op jit(solution)/shard_map/all_gather | solution.py:34
  42.9 169.9 %all-gather.8.cloned.1.call-start = ((), (), s32[]{:S(2)}) async-start(), calls=%async_computation.8 | async-start | bytes 3145728 | tf_op jit(solution)/shard_map/all_gather | solution.py:33
  43.5 209.7 %all-gather.12.cloned.1.call-start = ((), (), s32[]{:S(2)}) async-start(), calls=%async_computation.10 | async-start | bytes 3145728 | tf_op jit(solution)/shard_map/all_gather | solution.py:35
  44.1 275.3 %reduce-scatter.4.cloned.1.call-start = ((), (), s32[]{:S(2)}) async-start(), calls=%async_computation.11 | async-start | bytes 4718592 | tf_op jit(solution)/shard_map/reduce_scatter | solution.py:19
  253.1 4.4 copy-start.6
  260.9 1.6 copy-start.5
  260.9 122.2 %reduce-scatter.6.cloned.1.call-start = ((), (), s32[]{:S(2)}) async-start(), calls=%async_computation.13 | async-start | bytes 4718592 | tf_op jit(solution)/shard_map/reduce_scatter | solution.py:19
  262.5 1.6 copy-start.4
  267.4 203.4 %reduce-scatter.8.cloned.1.call-start = ((), (), s32[]{:S(2)}) async-start(), calls=%async_computation.14 | async-start | bytes 9437184 | tf_op jit(solution)/shard_map/reduce_scatter | solution.py:66
  267.6 3.7 copy-start.3
  321.4 63.7 %all-to-all-start.1 = ((bf16[16,4,4096]{2,1,0:T(4,128)(2,1)}), bf16[16,4,4096]{2,1,0:T(4,128)(2,1)S(1)}, u32[]{:S(2)}, u32[]{:S(2)}) async-start(bf16[16,4,4096]{2,1,0:T(4,128)(2,1)} %reshape.52), calls=%async_computation.2 | async-start | bytes 1048576 | tf_op jit(solution)/shard_map/all_to_all | solution.py:21
  385.1 19.0 %all-to-all-start.3 = ((bf16[16,4,4096]{2,1,0:T(4,128)(2,1)}), bf16[16,4,4096]{2,1,0:T(4,128)(2,1)}, u32[]{:S(2)}, u32[]{:S(2)}) async-start(bf16[16,4,4096]{2,1,0:T(4,128)(2,1)} %reshape.54), calls=%async_computation.5 | async-start | bytes 1048576 | tf_op jit(solution)/shard_map/all_to_all | solution.py:21
  470.8 8.1 %copy-start.1 = (bf16[128,4096]{1,0:T(8,128)(2,1)S(1)}, bf16[128,4096]{1,0:T(8,128)(2,1)}, u32[]{:S(2)}) copy-start(bf16[128,4096]{1,0:T(8,128)(2,1)} %param.7) | copy-start | bytes 3145732
Sparse Core Ops, SparseCore 0:
  27.6 50.8 all-gather.5
  80.4 51.1 all-gather.13
  133.4 38.9 all-gather.9
  174.1 38.6 all-gather.7
  214.4 38.6 all-gather.11
  261.0 58.3 reduce-scatter.3
  321.9 61.0 reduce-scatter.5
  385.6 85.1 reduce-scatter.7
where the time goes:
time: 487 us; the launch traced here: 486 us
  waiting for transfers between devices  349 us (72%)
  local copies, waits for them, and re-layouts  32.9 us (7%)
  blocking collectives  31 us (6%)
  matrix products  26.9 us (6%)
  other arithmetic  18.5 us (4%)
  between operations  14.3 us (3%)
  starting transfers between devices  13.2 us (3%)
    reduce_scatter x2, waiting for transfers between devices, bring_back(): lax.psum_scatter(partial_value, 'col', scatter_dimension=0, tiled=True)  91.5 us
    all_gather x2, waiting for transfers between devices, send_out(): shared = lax.all_gather(arrived, 'col', axis=0, tiled=True)  80.6 us
    reduce_scatter x1, waiting for transfers between devices, shards(): lax.psum_scatter(jnp.concatenate([lax.dot_general(token_rows, gate_rows,...  62 us
    all_gather x1, waiting for transfers between devices, shards(): lax.all_gather(gate_weight, 'dp', axis=1, tiled=True)  36.2 us
    all_gather x1, waiting for transfers between devices, shards(): lax.all_gather(down_weight, 'dp', axis=1, tiled=True)  36.2 us
    all_gather x1, waiting for transfers between devices, shards(): lax.all_gather(up_weight, 'dp', axis=1, tiled=True)  33.8 us
    all_to_all x2, blocking collectives, send_out(): lax.all_to_all(payload, 'yx', split_axis=0, concat_axis=0, tiled=True)  31 us
    reshape x2, local copies, waits for them, and re-layouts, send_out(): return shared.reshape(-1, payload.shape[-1])  13.8 us
  transfers between devices with their start and end apart: 10, of which 9 were waited for; matrix products, arithmetic and copies ran while one was open for 12% of the time, Pallas kernels for 0%

commit v1 on v0

--- a/solution.py
+++ b/solution.py
@@ -31,7 +31,9 @@
     contract_first = (((0,), (0,)), ((), ()))
     full_gate, full_up, full_down = (
         lax.all_gather(gate_weight, "dp", axis=1, tiled=True),
-        lax.all_gather(up_weight, "dp", axis=1, tiled=True),
+        jnp.concatenate(
+            lax.all_to_all(jnp.stack([up_weight] * lax.axis_size("dp")), "dp", 0, 0), axis=1
+        ),
         lax.all_gather(down_weight, "dp", axis=1, tiled=True),
     )
     full_gate = full_gate[0]

time: 487 us -> 460 us (0.945)
  waiting for transfers between devices: 349 us -> 317 us
    all_gather x1 -> x0, waiting for transfers between devices: 33.8 us -> none  [shards(): lax.all_gather(up_weight, 'dp', axis=1, tiled=True)]
    all_gather x2, waiting for transfers between devices: 80.6 us -> 89.3 us  [send_out(): shared = lax.all_gather(arrived, 'col', axis=0, tiled=True)]
    all_gather x1, waiting for transfers between devices: 36.2 us -> 29.6 us  [shards(): lax.all_gather(gate_weight, 'dp', axis=1, tiled=True)]
  transfers between devices with their start and end apart: 10 -> 10, of which waited for: 9 -> 8; matrix products, arithmetic and copies ran while one was open for 12% -> 14% of each run, Pallas kernels for 0% -> 0%
where the time goes in v1:
time: 460 us; the launch traced here: 459 us
  waiting for transfers between devices  317 us (69%)
  local copies, waits for them, and re-layouts  31.2 us (7%)
  blocking collectives  31 us (7%)
  matrix products  29.6 us (6%)
  other arithmetic  20 us (4%)
  starting transfers between devices  16.4 us (4%)
  between operations  14.3 us (3%)
    reduce_scatter x2, waiting for transfers between devices, bring_back(): lax.psum_scatter(partial_value, 'col', scatter_dimension=0, tiled=True)  91.9 us
    all_gather x2, waiting for transfers between devices, send_out(): shared = lax.all_gather(arrived, 'col', axis=0, tiled=True)  89.3 us
    reduce_scatter x1, waiting for transfers between devices, shards(): lax.psum_scatter(jnp.concatenate([lax.dot_general(token_rows, gate_rows,...  63.1 us
    all_gather x1, waiting for transfers between devices, shards(): lax.all_gather(down_weight, 'dp', axis=1, tiled=True)  35.4 us
    all_to_all x2, blocking collectives, send_out(): lax.all_to_all(payload, 'yx', split_axis=0, concat_axis=0, tiled=True)  31 us
    all_gather x1, waiting for transfers between devices, shards(): lax.all_gather(gate_weight, 'dp', axis=1, tiled=True)  29.6 us
    reshape x2, local copies, waits for them, and re-layouts, send_out(): return shared.reshape(-1, payload.shape[-1])  13.8 us
    all_to_all x2, starting transfers between devices, bring_back(): lax.all_to_all(summed, 'yx', split_axis=0, concat_axis=0, tiled=True)  12.1 us
  transfers between devices with their start and end apart: 10, of which 8 were waited for; matrix products, arithmetic and copies ran while one was open for 14% of the time, Pallas kernels for 0%

profile of v1, /device:TPU:1, one launch (start us, length us, event | category | flops | bytes accessed | tf_op | source)
XLA Modules:
  0.0 459.0 jit_solution(13513801458922401310)
XLA Ops:
  9.5 18.0 %all_to_all.25 = bf16[16,4,4096]{2,1,0:T(4,128)(2,1)} all-to-all(bf16[16,4,4096]{2,1,0:T(4,128)(2,1)S(1)} %reshape.56), channel_id=1, replica_groups=mesh['dp'=2,'yx'=16,'col'=8] {'yx'}, dimensions={0} | all-to-all | bytes 1048576 | tf_op jit(solution)/shard_map/all_to_all | solution.py:12
  29.2 13.0 %all_to_all.26 = bf16[16,4,4096]{2,1,0:T(4,128)(2,1)} all-to-all(bf16[16,4,4096]{2,1,0:T(4,128)(2,1)S(1)} %multiply_convert_fusion), channel_id=1, replica_groups=mesh['dp'=2,'yx'=16,'col'=8] {'yx'}, dimensions={0} | all-to-all | bytes 1048576 | tf_op jit(solution)/shard_map/all_to_all | solution.py:12
  44.4 3.8 all-to-all-start.1
  48.8 43.4 %all-gather.5.cloned.1.call-done = bf16[128,4,4096]{2,1,0:T(4,128)(2,1)} async-done(((bf16[16,4,4096]{2,1,0:T(4,128)(2,1)}), bf16[128,4,4096]{2,1,0:T(4,128)(2,1)}) %all-gather.5.cloned.1.call-update) | async-done | bytes 4194320 | tf_op jit(solution)/shard_map/all_gather | solution.py:13
  92.2 6.9 %reshape.51 = bf16[512,4096]{1,0:T(8,128)(2,1)} reshape(bf16[128,4,4096]{2,1,0:T(4,128)(2,1)} %all-gather.5.cloned.1.call-done) | data formatting | bytes 8388608 | tf_op jit(solution)/shard_map/reshape | solution.py:14
  99.1 45.9 %all-gather.11.cloned.1.call-done = bf16[128,4,4096]{2,1,0:T(4,128)(2,1)} async-done(((bf16[16,4,4096]{2,1,0:T(4,128)(2,1)}), bf16[128,4,4096]{2,1,0:T(4,128)(2,1)}) %all-gather.11.cloned.1.call-update) | async-done | bytes 4194320 | tf_op jit(solution)/shard_map/all_gather | solution.py:13
  145.0 6.9 %reshape.53 = bf16[512,4096]{1,0:T(8,128)(2,1)} reshape(bf16[128,4,4096]{2,1,0:T(4,128)(2,1)} %all-gather.11.cloned.1.call-done) | data formatting | bytes 8388608 | tf_op jit(solution)/shard_map/reshape | solution.py:14
  151.9 4.2 fusion.11
  156.2 29.6 %all-gather.7.cloned.1.call-done = bf16[1,4096,256]{2,1,0:T(8,128)(2,1)} async-done(((bf16[1,2048,256]{2,1,0:T(8,128)(2,1)}), bf16[1,4096,256]{2,1,0:T(8,128)(2,1)}) %all-gather.7.cloned.1.call-update) | async-done | bytes 2097168 | tf_op jit(solution)/shard_map/all_gather | solution.py:33
  185.8 4.9 %fusion.5 = f32[512,256]{1,0:T(8,128)} fusion(bf16[512,4096]{1,0:T(8,128)(2,1)} %reshape.51, bf16[1,4096,256]{2,1,0:T(8,128)(2,1)} %all-gather.7.cloned.1.call-done), kind=kOutput, calls=%fused_computation.16 | convolution fusion | flops 1073741824 | bytes 6815744 | tf_op jit(solution)/shard_map/dot_general | solution.py:45
  190.7 35.4 %all-gather.9.cloned.1.call-done = bf16[1,4096,256]{2,1,0:T(8,128)(2,1)} async-done(((bf16[1,2048,256]{2,1,0:T(8,128)(2,1)}), bf16[1,4096,256]{2,1,0:T(8,128)(2,1)}) %all-gather.9.cloned.1.call-update) | async-done | bytes 2097168 | tf_op jit(solution)/shard_map/all_gather | solution.py:37
  226.1 4.6 multiply_convert_fusion.1
  230.7 3.3 convolution_convert_fusion
  237.0 3.3 add_convert_fusion
  240.6 3.6 convolution_convert_fusion.1
  247.0 9.4 %pad_maximum_fusion = bf16[4096,768]{0,1:T(8,128)(2,1)} fusion(bf16[4096,256]{0,1:T(8,128)(2,1)S(1)} %convolution_convert_fusion.1, bf16[4096,256]{0,1:T(8,128)(2,1)S(1)} %convolution_convert_fusion.2, bf16[4096,256]{0,1:T(8,128)(2,1)S(1)} %convolution_convert_fusion.3), kind=kLoop, calls=%fused_computation.5 | loop fusion | flops 18874368 | bytes 12582912 | tf_op jit(solution)/shard_map/concatenate | solution.py:69
  256.4 36.2 %reduce-scatter.4.cloned.1.call-done = bf16[64,4096]{1,0:T(8,128)(2,1)} async-done(((bf16[512,4096]{1,0:T(8,128)(2,1)}), bf16[64,4096]{1,0:T(8,128)(2,1)}) %reduce-scatter.4.cloned.1.call-update) | async-done | bytes 524304 | tf_op jit(solution)/shard_map/reduce_scatter | solution.py:19
  294.6 5.9 %all-to-all-start.2 = ((bf16[16,4,4096]{2,1,0:T(4,128)(2,1)}), bf16[16,4,4096]{2,1,0:T(4,128)(2,1)S(1)}, u32[]{:S(2)}, u32[]{:S(2)}) async-start(bf16[16,4,4096]{2,1,0:T(4,128)(2,1)} %reshape.52), calls=%async_computation.3 | async-start | bytes 1048576 | tf_op jit(solution)/shard_map/all_to_all | solution.py:21
  300.6 55.7 %reduce-scatter.6.cloned.1.call-done = bf16[64,4096]{1,0:T(8,128)(2,1)} async-done(((bf16[512,4096]{1,0:T(8,128)(2,1)}), bf16[64,4096]{1,0:T(8,128)(2,1)}) %reduce-scatter.6.cloned.1.call-update) | async-done | bytes 524304 | tf_op jit(solution)/shard_map/reduce_scatter | solution.py:19
  358.3 6.2 %all-to-all-start.4 = ((bf16[16,4,4096]{2,1,0:T(4,128)(2,1)}), bf16[16,4,4096]{2,1,0:T(4,128)(2,1)}, u32[]{:S(2)}, u32[]{:S(2)}) async-start(bf16[16,4,4096]{2,1,0:T(4,128)(2,1)} %reshape.54), calls=%async_computation.6 | async-start | bytes 1048576 | tf_op jit(solution)/shard_map/all_to_all | solution.py:21
  366.1 3.1 scatter_custom_fusion
  370.3 6.0 %all-to-all-done.4 = bf16[16,4,4096]{2,1,0:T(4,128)(2,1)} async-done(((bf16[16,4,4096]{2,1,0:T(4,128)(2,1)}), bf16[16,4,4096]{2,1,0:T(4,128)(2,1)}, u32[]{:S(2)}, u32[]{:S(2)}) %all-to-all-start.4) | async-done | bytes 524320 | tf_op jit(solution)/shard_map/all_to_all | solution.py:21
  381.0 63.1 %reduce-scatter.8.cloned.1.call-done = bf16[2048,768]{0,1:T(8,128)(2,1)} async-done(((bf16[4096,768]{0,1:T(8,128)(2,1)}), bf16[2048,768]{0,1:T(8,128)(2,1)}) %reduce-scatter.8.cloned.1.call-update) | async-done | bytes 3145744 | tf_op jit(solution)/shard_map/reduce_scatter | solution.py:68
  444.1 3.1 slice_bitcast_fusion
  (55 shorter events, 29.0 us)
Async XLA Ops:
  7.2 1.2 copy-start
  7.2 85.0 %all-gather.5.cloned.1.call-start = ((), (), s32[]{:S(2)}) async-start(), calls=%async_computation.8 | async-start | bytes 4718592 | tf_op jit(solution)/shard_map/all_gather | solution.py:13
  8.4 19.2 %copy-start.6 = (f32[1,16,4]{1,2,0:T(4,128)S(1)}, f32[1,16,4]{1,2,0:T(4,128)}, u32[]{:S(2)}) copy-start(f32[1,16,4]{1,2,0:T(4,128)} %param.9) | copy-start | bytes 772
  8.4 19.2 %copy-start.2 = (bf16[128,4096]{1,0:T(8,128)(2,1)S(1)}, bf16[128,4096]{1,0:T(8,128)(2,1)}, u32[]{:S(2)}) copy-start(bf16[128,4096]{1,0:T(8,128)(2,1)} %param.13) | copy-start | bytes 3145732
  27.5 117.5 %all-gather.11.cloned.1.call-start = ((), (), s32[]{:S(2)}) async-start(), calls=%async_computation.12 | async-start | bytes 4718592 | tf_op jit(solution)/shard_map/all_gather | solution.py:13
  28.5 14.4 %copy-start.5 = (bf16[1,2048,256]{2,1,0:T(8,128)(2,1)S(1)}, bf16[1,2048,256]{2,1,0:T(8,128)(2,1)}, u32[]{:S(2)}) copy-start(bf16[1,2048,256]{2,1,0:T(8,128)(2,1)} %param.11) | copy-start | bytes 3145732
  42.2 143.6 %all-gather.7.cloned.1.call-start = ((), (), s32[]{:S(2)}) async-start(), calls=%async_computation.9 | async-start | bytes 3145728 | tf_op jit(solution)/shard_map/all_gather | solution.py:33
  44.4 107.5 %all-to-all-start.1 = ((bf16[2,1,2048,256]{3,2,1,0:T(8,128)(2,1)}), bf16[2,1,2048,256]{3,2,1,0:T(8,128)(2,1)S(1)}, u32[]{:S(2)}, u32[]{:S(2)}) async-start(bf16[2,1,2048,256]{3,2,1,0:T(8,128)(2,1)} %pad_maximum_fusion.1), calls=%async_computation.1 | async-start | bytes 4194304 | tf_op jit(solution)/shard_map/all_to_all | solution.py:35
  48.2 177.9 %all-gather.9.cloned.1.call-start = ((), (), s32[]{:S(2)}) async-start(), calls=%async_computation.10 | async-start | bytes 3145728 | tf_op jit(solution)/shard_map/all_gather | solution.py:37
  48.8 243.8 %reduce-scatter.4.cloned.1.call-start = ((), (), s32[]{:S(2)}) async-start(), calls=%async_computation.11 | async-start | bytes 4718592 | tf_op jit(solution)/shard_map/reduce_scatter | solution.py:19
  226.1 4.6 copy-start.4
  234.1 122.2 %reduce-scatter.6.cloned.1.call-start = ((), (), s32[]{:S(2)}) async-start(), calls=%async_computation.13 | async-start | bytes 4718592 | tf_op jit(solution)/shard_map/reduce_scatter | solution.py:19
  240.4 203.7 %reduce-scatter.8.cloned.1.call-start = ((), (), s32[]{:S(2)}) async-start(), calls=%async_computation.14 | async-start | bytes 9437184 | tf_op jit(solution)/shard_map/reduce_scatter | solution.py:68
  240.6 3.7 copy-start.3
  294.6 63.7 %all-to-all-start.2 = ((bf16[16,4,4096]{2,1,0:T(4,128)(2,1)}), bf16[16,4,4096]{2,1,0:T(4,128)(2,1)S(1)}, u32[]{:S(2)}, u32[]{:S(2)}) async-start(bf16[16,4,4096]{2,1,0:T(4,128)(2,1)} %reshape.52), calls=%async_computation.3 | async-start | bytes 1048576 | tf_op jit(solution)/shard_map/all_to_all | solution.py:21
  358.3 18.0 %all-to-all-start.4 = ((bf16[16,4,4096]{2,1,0:T(4,128)(2,1)}), bf16[16,4,4096]{2,1,0:T(4,128)(2,1)}, u32[]{:S(2)}, u32[]{:S(2)}) async-start(bf16[16,4,4096]{2,1,0:T(4,128)(2,1)} %reshape.54), calls=%async_computation.6 | async-start | bytes 1048576 | tf_op jit(solution)/shard_map/all_to_all | solution.py:21
  447.2 5.0 %copy-start.1 = (bf16[128,4096]{1,0:T(8,128)(2,1)S(1)}, bf16[128,4096]{1,0:T(8,128)(2,1)}, u32[]{:S(2)}) copy-start(bf16[128,4096]{1,0:T(8,128)(2,1)} %param.7) | copy-start | bytes 3145732
Sparse Core Ops, SparseCore 0:
  27.6 64.5 all-gather.4
  94.1 50.8 all-gather.10
  146.8 38.9 all-gather.6
  187.4 38.6 all-gather.8
  234.2 58.3 reduce-scatter.3
  295.0 61.2 reduce-scatter.5
  358.8 85.2 reduce-scatter.7
